TPU v7x, 128 devices: a whole 4x4x4 slice. The times are simulated.
128 devices in a mesh: req: 4 (over z), blk: 32 (over y, x, core).
Axes of the slice: x: 4, y: 4, z: 4, core: 2. Of those that a mesh axis runs over, the one named last changes fastest.
Arguments:
- tree_input: bfloat16 [6144, 1280], P(('req', 'blk')), may hold values from -6 to 6
- cache: bfloat16 [4, 2, 65536, 1280], P('req', None, 'blk'), may hold values from -1200 to 1200, as said below
- page_table: int32 [4, 512], P('req'), may hold values from 0 to 511, each once within a row
- lengths: int32 [4, 32], P('req'), may hold values from 1 to 32768, 57344 in all within a row
- parents: int32 [128, 48], P(('req', 'blk')), may hold values from 0 to 29, as said below
- accept_leaf: int32 [4, 32], P('req'), may hold values from 0 to 47
- w_qkv: bfloat16 [1280, 3840], P(None, 'blk'), may hold values from -0.15625 to 0.15625
- w_out: bfloat16 [1280, 1280], P(None, 'blk'), may hold values from -0.15625 to 0.15625
- w_up: bfloat16 [1280, 1280], P(None, 'blk'), may hold values from -0.15625 to 0.15625
- w_down: bfloat16 [1280, 1280], P('blk'), may hold values from -0.15625 to 0.15625
- w_draft: bfloat16 [4, 1280, 1280], P(None, None, 'blk'), may hold values from -0.15625 to 0.15625
- w_patch: bfloat16 [1280, 1280], P(None, 'req'), may hold values from -0.15625 to 0.15625
Outputs:
- layer_out: bfloat16 [6144, 1280], P(('req', 'blk'))
- drafts: bfloat16 [4, 6144, 1280], P(None, ('req', 'blk'))
- cache_new: bfloat16 [4, 2, 65536, 1280], P('req', None, 'blk')
Inputs may be any that keep to these rules, and one draw needn't show every extreme that they name: `cache`: keys of the pool may hold a few rows of far larger size. `parents`: node 0 is its own parent. The nodes form 5 levels of sizes 1, 4, 10, 15, 18 in index order, and every other node's parent lies in the level before its own. `page_table`: row g holds the pool pages of group g; request r's pages are the npages_r entries after those of requests before it (see the steps), and page p is held by index p // 16 of blk.
All inputs are finite; a program needn't handle non-finite values.
Results may differ from a plain program's by a relative error of at most 0.018.
The roundings to bfloat16 on the way count: a program that leaves them out, or rounds other values in their place, can miss the bound.
Values may be sent and summed in bfloat16 or wider, within the bound.
A program may use at most 192 MiB of HBM per device.

v0:
```python
import math
import jax
import jax.numpy as jnp
from jax import lax
from jax.sharding import PartitionSpec as P

H = 16
HD = 80
TREE = 48
DEPTH = 5
PAGE = 128
EPS = 1e-06
NEG = -1e30
LEVEL_START = (0, 1, 5, 15, 30, 48)


def rms_rows(values):
    wide = values.astype(jnp.float32)
    return (wide * lax.rsqrt(jnp.mean(wide * wide, axis=-1, keepdims=True) + EPS)).astype(
        jnp.bfloat16
    )


def ancestors(parent_rows):
    nodes = jnp.arange(TREE, dtype=jnp.int32)
    current = jnp.broadcast_to(nodes, parent_rows.shape)
    marks = current[:, :, None] == nodes[None, None, :]
    for level in range(DEPTH - 1):
        current = jnp.take_along_axis(parent_rows, current, axis=1)
        marks = marks | (current[:, :, None] == nodes[None, None, :])
    return marks


def row_blocks(values, mapper):
    return mapper(lax.all_gather(values, "blk", axis=0, tiled=True), jnp.int32(0))


def column_blocks(values):
    return lax.all_to_all(values, "blk", split_axis=0, concat_axis=1, tiled=True)


def on_device(
    tree_input,
    cache,
    page_table,
    lengths,
    parents,
    accept_leaf,
    w_qkv,
    w_out,
    w_up,
    w_down,
    w_draft,
    w_patch,
):
    blocks = lax.axis_size("blk")
    myself = lax.axis_index("blk")
    tree_rows = tree_input.shape[0]
    width = tree_input.shape[1]
    requests = lengths.shape[1]
    pool_pages = cache.shape[2] // PAGE
    scale = 1.0 / math.sqrt(HD)
    normed = rms_rows(tree_input)

    def project_qkv(piece, start):
        return jnp.dot(piece, w_qkv, preferred_element_type=jnp.float32).astype(jnp.bfloat16)

    projected_part = row_blocks(normed, project_qkv)
    projected = column_blocks(projected_part)
    key_own = projected[:, width : 2 * width]
    value_own = projected[:, 2 * width :]
    query_all = lax.all_gather(projected[:, :width], "blk", axis=0, tiled=True)
    page_row = page_table[0]
    length_row = lengths[0]
    leaf_row = accept_leaf[0]
    total_pages = page_row.shape[0]
    npages = (length_row + DEPTH + PAGE - 1) // PAGE
    page_ends = jnp.cumsum(npages)
    offsets = page_ends - npages
    local_ids = myself * pool_pages + jnp.arange(pool_pages, dtype=jnp.int32)
    located = page_row[None, :] == local_ids[:, None]
    where_at = jnp.sum(
        jnp.where(located, jnp.arange(total_pages, dtype=jnp.int32)[None, :], 0), axis=1
    )
    owner = jnp.sum((page_ends[None, :] <= where_at[:, None]).astype(jnp.int32), axis=1)
    owner_hot = owner[:, None] == jnp.arange(requests, dtype=jnp.int32)[None, :]
    safe_owner = jnp.minimum(owner, requests - 1)
    page_len = jnp.sum(jnp.where(owner_hot, length_row[None, :], 0), axis=1)
    page_offset = jnp.sum(jnp.where(owner_hot, offsets[None, :], 0), axis=1)
    positions = (where_at - page_offset)[:, None] * PAGE + jnp.arange(PAGE, dtype=jnp.int32)[
        None, :
    ]
    valid = positions < page_len[:, None]
    query4 = query_all.reshape(requests, tree_rows, H, HD)
    query_page = jnp.take(query4, safe_owner, axis=0)
    keys = cache[0, 0].reshape(pool_pages, PAGE, H, HD)
    values = cache[0, 1].reshape(pool_pages, PAGE, H, HD)
    scores = (
        jnp.einsum("pqhd,pthd->pqht", query_page, keys, preferred_element_type=jnp.float32) * scale
    )
    masked = jnp.where(valid[:, None, None, :], scores, NEG)
    page_max = jnp.max(masked, axis=-1)
    request_max = jnp.max(jnp.where(owner_hot.T[:, :, None, None], page_max[None], NEG), axis=1)
    page_top = jnp.take(request_max, safe_owner, axis=0)
    weights = jnp.where(valid[:, None, None, :], jnp.exp(masked - page_top[..., None]), 0.0)
    page_den = jnp.sum(weights, axis=-1)
    page_num = jnp.einsum(
        "pqht,pthd->pqhd", weights.astype(jnp.bfloat16), values, preferred_element_type=jnp.float32
    )
    hot = owner_hot.astype(jnp.float32)
    den_part = jnp.einsum("pr,pqh->rqh", hot, page_den, precision=lax.Precision.HIGHEST)
    num_part = jnp.einsum("pr,pqhd->rqhd", hot, page_num, precision=lax.Precision.HIGHEST).reshape(
        requests, tree_rows, width
    )
    max_all = lax.pmax(request_max, "blk")
    factor = jnp.exp(request_max - max_all)
    den_scaled = den_part * factor
    num_scaled = (num_part.reshape(requests, tree_rows, H, HD) * factor[..., None]).reshape(
        requests, tree_rows, width
    )
    den_own, num_own = (
        lax.psum_scatter(den_scaled, "blk", scatter_dimension=0, tiled=True),
        lax.psum_scatter(num_scaled, "blk", scatter_dimension=0, tiled=True),
    )
    cache_top = lax.dynamic_slice_in_dim(max_all, myself, 1, 0)[0]
    cache_den = den_own[0]
    cache_num = num_own[0]
    marks = ancestors(parents)[0]
    query_own = lax.dynamic_slice_in_dim(query_all, myself * tree_rows, tree_rows, 0).reshape(
        tree_rows, H, HD
    )
    key_tree = key_own.reshape(tree_rows, H, HD)
    value_tree = value_own.reshape(tree_rows, H, HD)
    tree_scores = (
        jnp.einsum("qhd,khd->qhk", query_own, key_tree, preferred_element_type=jnp.float32) * scale
    )
    tree_masked = jnp.where(marks[:, None, :], tree_scores, NEG)
    row_top = jnp.maximum(cache_top, jnp.max(tree_masked, axis=-1))
    tree_weights = jnp.where(marks[:, None, :], jnp.exp(tree_masked - row_top[..., None]), 0.0)
    carried = jnp.exp(cache_top - row_top)
    denom = cache_den * carried + jnp.sum(tree_weights, axis=-1)
    numer = cache_num.reshape(tree_rows, H, HD) * carried[..., None] + jnp.einsum(
        "qhk,khd->qhd",
        tree_weights.astype(jnp.bfloat16),
        value_tree,
        preferred_element_type=jnp.float32,
    )
    attended = (numer / denom[..., None]).reshape(tree_rows, width).astype(jnp.bfloat16)

    def project_out(piece, start):
        return jnp.dot(piece, w_out, preferred_element_type=jnp.float32).astype(jnp.bfloat16)

    proj = column_blocks(row_blocks(attended, project_out))
    mid = (tree_input.astype(jnp.float32) + proj.astype(jnp.float32)).astype(jnp.bfloat16)

    def project_up(piece, start):
        return jax.nn.gelu(jnp.dot(piece, w_up, preferred_element_type=jnp.float32)).astype(
            jnp.bfloat16
        )

    hidden_all = row_blocks(rms_rows(mid), project_up)
    feedforward = lax.psum_scatter(
        jnp.dot(hidden_all, w_down, preferred_element_type=jnp.float32),
        "blk",
        scatter_dimension=0,
        tiled=True,
    )
    layer_out = (mid.astype(jnp.float32) + feedforward).astype(jnp.bfloat16)
    head_count = w_draft.shape[0]
    head_cols = w_draft.shape[2]

    def project_draft(piece, start):
        grown = jnp.einsum("nd,kdc->nkc", piece, w_draft, preferred_element_type=jnp.float32)
        return (
            jax.nn.silu(grown).astype(jnp.bfloat16).reshape(piece.shape[0], head_count * head_cols)
        )

    branch = column_blocks(row_blocks(rms_rows(layer_out), project_draft))
    branch = (
        branch.reshape(tree_rows, blocks, head_count, head_cols)
        .transpose(2, 0, 1, 3)
        .reshape(head_count, tree_rows, width)
    )
    drafted = (layer_out.astype(jnp.float32)[None] + branch.astype(jnp.float32)).astype(
        jnp.bfloat16
    )
    drafts = jnp.einsum(
        "krd,do->kro",
        drafted,
        lax.all_gather(w_patch, "req", axis=1, tiled=True),
        preferred_element_type=jnp.float32,
    ).astype(jnp.bfloat16)
    my_leaf = lax.dynamic_slice_in_dim(leaf_row, myself, 1, 0)
    chosen = jnp.take(marks, my_leaf, axis=0)[0]
    ranks = jnp.cumsum(chosen.astype(jnp.int32)) - 1
    picker = chosen[None, :] & (ranks[None, :] == jnp.arange(DEPTH, dtype=jnp.int32)[:, None])
    both_rows = jnp.concatenate([key_own, value_own], axis=1)
    send_rows = jnp.dot(
        picker.astype(jnp.bfloat16), both_rows, preferred_element_type=jnp.float32
    ).astype(jnp.bfloat16)
    received = lax.all_gather(send_rows, "blk", axis=0, tiled=True)
    level_marks = jnp.asarray(LEVEL_START[1:-1], jnp.int32)
    accepted_count = 1 + jnp.sum(
        (leaf_row[:, None] >= level_marks[None, :]).astype(jnp.int32), axis=1
    )
    steps_ahead = jnp.arange(DEPTH, dtype=jnp.int32)
    written = length_row[:, None] + steps_ahead[None, :]
    page_index = jnp.take(
        page_row, jnp.clip(offsets[:, None] + written // PAGE, 0, total_pages - 1)
    )
    keeper = (steps_ahead[None, :] < accepted_count[:, None]) & (page_index // pool_pages == myself)
    target = jnp.where(
        keeper, page_index % pool_pages * PAGE + written % PAGE, pool_pages * PAGE
    ).reshape(-1)
    new_keys = cache[0, 0].at[target].set(received[:, :width], mode="drop")
    new_values = cache[0, 1].at[target].set(received[:, width:], mode="drop")
    cache_new = jnp.stack([new_keys, new_values])[None]
    return (layer_out, drafts, cache_new)


def solution(mesh):
    in_specs = (
        P(("req", "blk"), None),
        P("req", None, "blk", None),
        P("req", None),
        P("req", None),
        P(("req", "blk"), None),
        P("req", None),
        P(None, "blk"),
        P(None, "blk"),
        P(None, "blk"),
        P("blk", None),
        P(None, None, "blk"),
        P(None, "req"),
    )
    out_specs = (
        P(("req", "blk"), None),
        P(None, ("req", "blk"), None),
        P("req", None, "blk", None),
    )
    return jax.shard_map(
        on_device, mesh=mesh, in_specs=in_specs, out_specs=out_specs, check_vma=False
    )
```

profile of v0, /device:TPU:1, one launch (start us, length us, event | category | flops | bytes accessed | tf_op | source)
XLA Modules:
  0.0 739.8 jit_solution(1722064064987440074)
XLA Ops:
  10.0 50.1 %all-gather.8.cloned.1.call-done = bf16[1536,1280]{1,0:T(8,128)(2,1)} async-done(((bf16[48,1280]{1,0:T(8,128)(2,1)}), bf16[1536,1280]{1,0:T(8,128)(2,1)}) %all-gather.8.cloned.1.call-update) | async-done | bytes 3932176 | tf_op jit(solution)/shard_map/all_gather | solution.py:35
  63.9 15.2 %all_to_all.45 = bf16[32,48,120]{2,1,0:T(8,128)(2,1)S(1)} all-to-all(bf16[32,48,120]{2,1,0:T(8,128)(2,1)S(1)} %bitcast.182), channel_id=1, replica_groups=mesh['req'=4,'blk'=32] {'blk'}, dimensions={0} | all-to-all | bytes 737280 | tf_op jit(solution)/shard_map/all_to_all | solution.py:39
  81.0 10.6 %slice_bitcast_fusion.1 = (bf16[2048,1280]{1,0:T(8,128)(2,1)}, bf16[2048,1280]{1,0:T(8,128)(2,1)}, bf16[1,1,2048,1280]{3,2,1,0:T(8,128)(2,1)}, bf16[1,1,2048,1280]{3,2,1,0:T(8,128)(2,1)}) fusion(bf16[1,2,2048,1280]{3,2,1,0:T(8,128)(2,1)} %param.16), kind=kLoop, calls=%fused_computation.218 | loop fusion | bytes 31457280 | tf_op jit(solution)/shard_map/squeeze | solution.py:215
  91.6 15.7 %reshape.1047 = bf16[16,128,16,80]{3,2,1,0:T(8,128)(2,1)} reshape(bf16[1,1,2048,1280]{3,2,1,0:T(8,128)(2,1)} %get-tuple-element.30) | data formatting | bytes 10485760 | tf_op jit(solution)/shard_map/reshape;squeeze | solution.py:96
  107.3 15.8 %reshape.1048 = bf16[16,128,16,80]{3,2,1,0:T(8,128)(2,1)} reshape(bf16[1,1,2048,1280]{3,2,1,0:T(8,128)(2,1)} %get-tuple-element.29) | data formatting | bytes 10485760 | tf_op jit(solution)/shard_map/reshape;squeeze | solution.py:97
  124.2 12.1 %reshape.896 = bf16[32,48,16,80]{3,2,1,0:T(8,128)(2,1)} reshape(bf16[1536,1280]{1,0:T(8,128)(2,1)} %all-gather.10.cloned.1.call-done) | data formatting | bytes 7864320 | tf_op jit(solution)/shard_map/reshape | solution.py:94
  143.9 10.6 %bitcast_reduce_fusion = (f32[16,48,16]{1,2,0:T(8,128)S(1)}, f32[16,16,48,128]{3,2,1,0:T(8,128)}) fusion(pred[16,128]{1,0:T(8,128)(4,1)S(1)} %add_compare_fusion, bf16[16,128,16,80]{3,2,1,0:T(8,128)(2,1)} %reshape.1047, bf16[16,48,16,80]{3,2,1,0:T(8,128)(2,1)S(1)} %broadcast_select_fusion), kind=kOutput, calls=%fused_computation.15 | convolution fusion | flops 256364544 | bytes 13551616 | tf_op jit(solution)/shard_map/pqhd,pthd->pqht/dot_general | solution.py:99
  157.2 9.4 %fusion.23 = f32[16,48,16,80]{3,1,2,0:T(8,128)} fusion(bf16[16,128,16,80]{3,2,1,0:T(8,128)(2,1)} %reshape.1048, f32[16,16,48,128]{3,2,1,0:T(8,128)} %get-tuple-element.38, f32[16,48,16]{1,2,0:T(8,128)S(1)} %broadcast_select_fusion.1, pred[16,128]{1,0:T(8,128)(4,1)S(1)} %add_compare_fusion), kind=kOutput, calls=%fused_computation.37 | convolution fusion | flops 259522560 | bytes 15517696 | tf_op jit(solution)/shard_map/pqht,pthd->pqhd/dot_general | solution.py:107
  170.3 86.9 %all-reduce.2.cloned.1.call-done = f32[32,48,16]{1,0,2:T(8,128)} async-done(((f32[32,48,16]{1,0,2:T(8,128)}), f32[32,48,16]{1,0,2:T(8,128)}) %all-reduce.2.cloned.1.call-update) | async-done | bytes 98320 | tf_op jit(solution)/shard_map/pmax | solution.py:115
  259.9 13.2 %broadcast_multiply_fusion = f32[32,48,16,80]{3,0,2,1:T(8,128)} fusion(f32[32,48,16]{0,2,1:T(8,128)S(1)} %copy.110, f32[16,48,16,80]{3,1,2,0:T(8,128)} %fusion.23, s32[16]{0:T(128)S(1)} %convert_reduce_fusion), kind=kOutput, calls=%fused_computation.20 | convolution fusion | flops 379453952 | bytes 11894848 | tf_op jit(solution)/shard_map/pr,pqhd->rqhd/dot_general | solution.py:112
  273.0 16.4 %copy.111 = f32[32,48,16,80]{3,2,1,0:T(8,128)} copy(f32[32,48,16,80]{3,0,2,1:T(8,128)} %broadcast_multiply_fusion) | data formatting | bytes 15728640 | tf_op jit(solution)/shard_map/mul | solution.py:118
  289.5 12.8 %reshape.897 = f32[32,48,1280]{2,1,0:T(8,128)} reshape(f32[32,48,16,80]{3,2,1,0:T(8,128)} %copy.111) | data formatting | bytes 15728640 | tf_op jit(solution)/shard_map/reshape | solution.py:118
  309.3 26.3 %reduce-scatter.6.cloned.1.call-done = f32[1,48,16]{1,2,0:T(8,128)} async-done(((f32[32,48,16]{1,2,0:T(8,128)}), f32[1,48,16]{1,2,0:T(8,128)}) %reduce-scatter.6.cloned.1.call-update) | async-done | bytes 3088 | tf_op jit(solution)/shard_map/reduce_scatter | solution.py:122
  336.4 93.1 %reduce-scatter.4.cloned.1.call-done = f32[1,48,1280]{2,1,0:T(8,128)} async-done(((f32[32,48,1280]{2,1,0:T(8,128)}), f32[1,48,1280]{2,1,0:T(8,128)}) %reduce-scatter.4.cloned.1.call-update) | async-done | bytes 245776 | tf_op jit(solution)/shard_map/reduce_scatter | solution.py:123
  432.1 47.4 %all-gather.12.cloned.1.call-done = bf16[1536,1280]{1,0:T(8,128)(2,1)} async-done(((bf16[48,1280]{1,0:T(8,128)(2,1)}), bf16[1536,1280]{1,0:T(8,128)(2,1)}) %all-gather.12.cloned.1.call-update) | async-done | bytes 3932176 | tf_op jit(solution)/shard_map/all_gather | solution.py:35
  483.8 12.7 %all_to_all.46 = bf16[32,2,960]{2,1,0:T(2,128)(2,1)S(1)} all-to-all(bf16[32,2,960]{2,1,0:T(2,128)(2,1)S(1)} %reshape.1056), channel_id=1, replica_groups=mesh['req'=4,'blk'=32] {'blk'}, dimensions={0} | all-to-all | bytes 245760 | tf_op jit(solution)/shard_map/all_to_all | solution.py:39
  498.2 43.7 %all-gather.14.cloned.1.call-done = bf16[1536,1280]{1,0:T(8,128)(2,1)} async-done(((bf16[48,1280]{1,0:T(8,128)(2,1)}), bf16[1536,1280]{1,0:T(8,128)(2,1)}) %all-gather.14.cloned.1.call-update) | async-done | bytes 3932176 | tf_op jit(solution)/shard_map/all_gather | solution.py:35
  541.9 7.8 %fusion.66 = f32[1536,1280]{1,0:T(8,128)} fusion(bf16[40,1280]{1,0:T(8,128)(2,1)S(1)} %copy-done.7, bf16[1536,1280]{1,0:T(8,128)(2,1)} %all-gather.14.cloned.1.call-done, bf16[1280,40]{0,1:T(8,128)(2,1)S(1)} %copy-done.8), kind=kOutput, calls=%fused_computation.93 | convolution fusion | flops 315125760 | bytes 12001280 | tf_op jit(solution)/shard_map/dot_general | solution.py:163
  549.8 87.3 %reduce-scatter.8.cloned.1.call-done = f32[48,1280]{1,0:T(8,128)} async-done(((f32[1536,1280]{1,0:T(8,128)}), f32[48,1280]{1,0:T(8,128)}) %reduce-scatter.8.cloned.1.call-update) | async-done | bytes 245776 | tf_op jit(solution)/shard_map/reduce_scatter | solution.py:162
  645.3 26.9 %all-gather = bf16[32,5,2560]{2,1,0:T(8,128)(2,1)S(1)} all-gather(bf16[1,5,2560]{2,1,0:T(8,128)(2,1)S(1)} %fusion.12), channel_id=1, replica_groups=mesh['req'=4,'blk'=32] {'blk'}, dimensions={0}, use_global_device_ids=true | all-gather | bytes 844800 | tf_op jit(solution)/shard_map/all_gather | solution.py:201
  672.6 7.1 scatter_custom_fusion
  679.7 7.3 scatter_custom_fusion.1
  694.5 5.6 all-to-all-start.2
  700.1 9.1 %maximum_bitcast_fusion = bf16[1,2,2048,1280]{3,2,1,0:T(8,128)(2,1)} fusion(bf16[1,2048,1280]{2,1,0:T(8,128)(2,1)} %bitcast.177, bf16[1,2048,1280]{2,1,0:T(8,128)(2,1)} %bitcast.178), kind=kLoop, calls=%fused_computation.9 | loop fusion | flops 5242880 | bytes 20971520 | tf_op jit(solution)/shard_map/broadcast_in_dim | solution.py:217
  (164 shorter events, 79.8 us)
Async XLA Ops:
  7.2 680.3 %copy-start = (bf16[4,1280,40]{1,2,0:T(8,128)(2,1)S(1)}, bf16[4,1280,40]{1,2,0:T(8,128)(2,1)}, u32[]{:S(2)}) copy-start(bf16[4,1280,40]{1,2,0:T(8,128)(2,1)} %param.25) | copy-start | bytes 1228804
  7.2 53.0 %all-gather.8.cloned.1.call-start = ((), (), s32[]{:S(2)}) async-start(), calls=%async_computation.6 | async-start | bytes 4055040 | tf_op jit(solution)/shard_map/all_gather | solution.py:35
  8.3 72.4 %copy-start.9 = (s32[1,32]{1,0:T(1,128)S(1)}, s32[1,32]{1,0:T(1,128)}, u32[]{:S(2)}) copy-start(s32[1,32]{1,0:T(1,128)} %param.18) | copy-start | bytes 388
  10.0 114.2 %all-gather.10.cloned.1.call-start = ((), (), s32[]{:S(2)}) async-start(), calls=%async_computation.7 | async-start | bytes 4055040 | tf_op jit(solution)/shard_map/all_gather | solution.py:72
  80.5 176.7 %all-reduce.2.cloned.1.call-start = ((), (), s32[]{:S(2)}) async-start(), calls=%async_computation.8 | async-start | bytes 524288 | tf_op jit(solution)/shard_map/pmax | solution.py:115
  107.3 15.8 %copy-start.1 = (s32[1,512]{1,0:T(1,128)S(1)}, s32[1,512]{1,0:T(1,128)}, u32[]{:S(2)}) copy-start(s32[1,512]{1,0:T(1,128)} %param.17) | copy-start | bytes 6148
  156.8 9.8 %slice-start = ((s8[6291456]{0:T(1024)(128)(4,1)}), s8[2097152]{0:T(1024)(128)(4,1)S(1)}, s32[]{:S(2)}) async-start(s8[6291456]{0:T(1024)(128)(4,1)} %bitcast.175), calls=%async_computation.16 | async-start | bytes 4194304
  156.9 178.8 %reduce-scatter.6.cloned.1.call-start = ((), (), s32[]{:S(2)}) async-start(), calls=%async_computation.10 | async-start | bytes 270336 | tf_op jit(solution)/shard_map/reduce_scatter | solution.py:122
  157.2 9.5 %slice-start.1 = ((s8[6291456]{0:T(1024)(128)(4,1)}), s8[4194304]{0:T(1024)(128)(4,1)S(1)}, s32[]{:S(2)}) async-start(s8[6291456]{0:T(1024)(128)(4,1)} %bitcast.175), calls=%async_computation.17 | async-start | bytes 8388608
  259.8 169.7 %reduce-scatter.4.cloned.1.call-start = ((), (), s32[]{:S(2)}) async-start(), calls=%async_computation.9 | async-start | bytes 8110080 | tf_op jit(solution)/shard_map/reduce_scatter | solution.py:123
  302.3 4.0 copy-start.5
  302.3 177.3 %copy-start.6 = (bf16[1280,40]{0,1:T(8,128)(2,1)S(1)}, bf16[1280,40]{0,1:T(8,128)(2,1)}, u32[]{:S(2)}) copy-start(bf16[1280,40]{0,1:T(8,128)(2,1)} %param.22) | copy-start | bytes 307204
  302.3 177.2 %all-gather.12.cloned.1.call-start = ((), (), s32[]{:S(2)}) async-start(), calls=%async_computation.11 | async-start | bytes 4055040 | tf_op jit(solution)/shard_map/all_gather | solution.py:35
  431.1 66.1 %copy-start.3 = (bf16[48,1280]{1,0:T(8,128)(2,1)S(1)}, bf16[48,1280]{1,0:T(8,128)(2,1)}, u32[]{:S(2)}) copy-start(bf16[48,1280]{1,0:T(8,128)(2,1)} %param.15) | copy-start | bytes 368644
  432.0 109.9 %copy-start.7 = (bf16[40,1280]{1,0:T(8,128)(2,1)S(1)}, bf16[40,1280]{1,0:T(8,128)(2,1)}, u32[]{:S(2)}) copy-start(bf16[40,1280]{1,0:T(8,128)(2,1)} %param.24) | copy-start | bytes 307204
  432.1 109.9 %copy-start.8 = (bf16[1280,40]{0,1:T(8,128)(2,1)S(1)}, bf16[1280,40]{0,1:T(8,128)(2,1)}, u32[]{:S(2)}) copy-start(bf16[1280,40]{0,1:T(8,128)(2,1)} %param.23) | copy-start | bytes 307204
  432.1 109.8 %all-gather.14.cloned.1.call-start = ((), (), s32[]{:S(2)}) async-start(), calls=%async_computation.12 | async-start | bytes 4055040 | tf_op jit(solution)/shard_map/all_gather | solution.py:35
  498.1 138.9 %reduce-scatter.8.cloned.1.call-start = ((), (), s32[]{:S(2)}) async-start(), calls=%async_computation.13 | async-start | bytes 8110080 | tf_op jit(solution)/shard_map/reduce_scatter | solution.py:162
  549.7 89.8 %copy-start.10 = (s32[1,32]{1,0:T(1,128)S(1)}, s32[1,32]{1,0:T(1,128)}, u32[]{:S(2)}) copy-start(s32[1,32]{1,0:T(1,128)} %param.20) | copy-start | bytes 388
  549.7 137.7 %all-gather.16.cloned.1.call-start = ((), (), s32[]{:S(2)}) async-start(), calls=%async_computation.14 | async-start | bytes 4055040 | tf_op jit(solution)/shard_map/all_gather | solution.py:35
  638.0 6.1 copy-start.4
  638.9 89.9 %all-gather.18.cloned.1.call-start = ((), (), s32[]{:S(2)}) async-start(), calls=%async_computation.15 | async-start | bytes 4096000 | tf_op jit(solution)/shard_map/all_gather | solution.py:190
  642.5 2.0 copy-start.11
  694.5 19.8 %all-to-all-start.2 = ((bf16[32,48,160]{2,1,0:T(8,128)(2,1)}), bf16[32,48,160]{2,1,0:T(8,128)(2,1)S(1)}, u32[]{:S(2)}, u32[]{:S(2)}) async-start(bf16[32,48,160]{2,1,0:T(8,128)(2,1)} %copy.123), calls=%async_computation.5 | async-start | bytes 1572864 | tf_op jit(solution)/shard_map/all_to_all | solution.py:39
  (1 other events, 0.7 us)
Sparse Core Ops, SparseCore 0:
  10.8 49.2 all-gather.7
  80.6 43.5 all-gather.9
  157.0 100.1 all-reduce.1
  261.1 74.5 reduce-scatter.5
  339.9 89.5 reduce-scatter.3
  432.4 47.0 all-gather.11
  498.2 43.6 all-gather.13
  549.8 87.1 reduce-scatter.7
  639.9 47.5 all-gather.15
  688.9 39.8 all-gather.17
where the time goes:
time: 744 us; the launch traced here: 740 us
  waiting for transfers between devices  445 us (60%)
  local copies, waits for them, and re-layouts  135 us (18%)
  matrix products  56.5 us (8%)
  blocking collectives  54.9 us (7%)
  other arithmetic  25.4 us (3%)
  between operations  16.9 us (2%)
    all_gather x4, waiting for transfers between devices, row_blocks(): lax.all_gather(values, 'blk', axis=0, tiled=True)  142 us
    reduce_scatter x1, waiting for transfers between devices, on_device(): lax.psum_scatter(num_scaled, 'blk', scatter_dimension=0, tiled=True)  93.1 us
    reduce_scatter x1, waiting for transfers between devices, on_device(): lax.psum_scatter(jnp.dot(hidden_all, w_down, preferred_element_type=jnp.f...  87.3 us
    pmax x1, waiting for transfers between devices, on_device(): max_all = lax.pmax(request_max, 'blk')  86.9 us
    all_to_all x2, blocking collectives, column_blocks(): lax.all_to_all(values, 'blk', split_axis=0, concat_axis=1, tiled=True)  27.9 us
    all_gather x1, blocking collectives, on_device(): received = lax.all_gather(send_rows, 'blk', axis=0, tiled=True)  26.9 us
    reduce_scatter x1, waiting for transfers between devices, on_device(): lax.psum_scatter(den_scaled, 'blk', scatter_dimension=0, tiled=True)  26.3 us
    mul x1, local copies, waits for them, and re-layouts, on_device(): num_part.reshape(requests, tree_rows, H, HD) * factor[..., None]  16.4 us
  transfers between devices with their start and end apart: 11, of which 11 were waited for; matrix products, arithmetic and copies ran while one was open for 20% of the time, Pallas kernels for 0%

commit v1 on v0

--- a/solution.py
+++ b/solution.py
@@ -32,7 +32,12 @@
 
 
 def row_blocks(values, mapper):
-    return mapper(lax.all_gather(values, "blk", axis=0, tiled=True), jnp.int32(0))
+    return mapper(
+        jnp.concatenate(
+            lax.all_to_all(jnp.stack([values] * lax.axis_size("blk")), "blk", 0, 0), axis=0
+        ),
+        jnp.int32(0),
+    )
 
 
 def column_blocks(values):

time: 744 us -> 798 us (1.073)
  blocking collectives: 54.9 us -> 248 us
  waiting for transfers between devices: 445 us -> 298 us
    all_to_all x0 -> x3, blocking collectives: none -> 163 us  [row_blocks(): lax.all_to_all(jnp.stack([values] * lax.axis_size('blk')), 'blk', 0, 0)]
    all_gather x4 -> x0, waiting for transfers between devices: 142 us -> none  [row_blocks(): lax.all_gather(values, 'blk', axis=0, tiled=True)]
    all_gather x1, blocking collectives: 26.9 us -> 59.5 us  [on_device(): received = lax.all_gather(send_rows, 'blk', axis=0, tiled=True)]
  transfers between devices with their start and end apart: 11 -> 8, of which waited for: 11 -> 6; matrix products, arithmetic and copies ran while one was open for 20% -> 19% of each run, Pallas kernels for 0% -> 0%
where the time goes in v1:
time: 798 us; the launch traced here: 793 us
  waiting for transfers between devices  298 us (37%)
  blocking collectives  248 us (31%)
  local copies, waits for them, and re-layouts  137 us (17%)
  matrix products  52.1 us (7%)
  other arithmetic  26.2 us (3%)
  between operations  18 us (2%)
  starting transfers between devices  14 us (2%)
    all_to_all x3, blocking collectives, row_blocks(): lax.all_to_all(jnp.stack([values] * lax.axis_size('blk')), 'blk', 0, 0)  163 us
    reduce_scatter x1, waiting for transfers between devices, on_device(): lax.psum_scatter(num_scaled, 'blk', scatter_dimension=0, tiled=True)  93.1 us
    reduce_scatter x1, waiting for transfers between devices, on_device(): lax.psum_scatter(jnp.dot(hidden_all, w_down, preferred_element_type=jnp.f...  86.5 us
    pmax x1, waiting for transfers between devices, on_device(): max_all = lax.pmax(request_max, 'blk')  84.9 us
    all_gather x1, blocking collectives, on_device(): received = lax.all_gather(send_rows, 'blk', axis=0, tiled=True)  59.5 us
    reduce_scatter x1, waiting for transfers between devices, on_device(): lax.psum_scatter(den_scaled, 'blk', scatter_dimension=0, tiled=True)  26.5 us
    all_to_all x2, blocking collectives, column_blocks(): lax.all_to_all(values, 'blk', split_axis=0, concat_axis=1, tiled=True)  25.1 us
    mul x1, local copies, waits for them, and re-layouts, on_device(): num_part.reshape(requests, tree_rows, H, HD) * factor[..., None]  16.4 us
  transfers between devices with their start and end apart: 8, of which 6 were waited for; matrix products, arithmetic and copies ran while one was open for 19% of the time, Pallas kernels for 0%

profile of v1, /device:TPU:1, one launch (start us, length us, event | category | flops | bytes accessed | tf_op | source)
XLA Modules:
  0.0 792.8 jit_solution(12654976365805552666)
XLA Ops:
  10.4 56.3 %all_to_all.65 = bf16[32,48,1280]{2,1,0:T(8,128)(2,1)S(1)} all-to-all(bf16[32,48,1280]{2,1,0:T(8,128)(2,1)S(1)} %stack.14), channel_id=1, replica_groups=mesh['req'=4,'blk'=32] {'blk'}, dimensions={0} | all-to-all | bytes 7864320 | tf_op jit(solution)/shard_map/all_to_all | solution.py:37
  68.3 13.8 %all_to_all.66 = bf16[32,48,120]{2,1,0:T(8,128)(2,1)S(1)} all-to-all(bf16[32,48,120]{2,1,0:T(8,128)(2,1)S(1)} %bitcast.187), channel_id=1, replica_groups=mesh['req'=4,'blk'=32] {'blk'}, dimensions={0} | all-to-all | bytes 737280 | tf_op jit(solution)/shard_map/all_to_all | solution.py:44
  84.0 10.6 %slice_bitcast_fusion.1 = (bf16[2048,1280]{1,0:T(8,128)(2,1)}, bf16[2048,1280]{1,0:T(8,128)(2,1)}, bf16[1,1,2048,1280]{3,2,1,0:T(8,128)(2,1)}, bf16[1,1,2048,1280]{3,2,1,0:T(8,128)(2,1)}) fusion(bf16[1,2,2048,1280]{3,2,1,0:T(8,128)(2,1)} %param.16), kind=kLoop, calls=%fused_computation.218 | loop fusion | bytes 31457280 | tf_op jit(solution)/shard_map/squeeze | solution.py:220
  94.6 15.7 %reshape.1072 = bf16[16,128,16,80]{3,2,1,0:T(8,128)(2,1)} reshape(bf16[1,1,2048,1280]{3,2,1,0:T(8,128)(2,1)} %get-tuple-element.30) | data formatting | bytes 10485760 | tf_op jit(solution)/shard_map/reshape;squeeze | solution.py:101
  110.3 15.8 %reshape.1073 = bf16[16,128,16,80]{3,2,1,0:T(8,128)(2,1)} reshape(bf16[1,1,2048,1280]{3,2,1,0:T(8,128)(2,1)} %get-tuple-element.29) | data formatting | bytes 10485760 | tf_op jit(solution)/shard_map/reshape;squeeze | solution.py:102
  128.1 12.1 %reshape.918 = bf16[32,48,16,80]{3,2,1,0:T(8,128)(2,1)} reshape(bf16[1536,1280]{1,0:T(8,128)(2,1)} %all-gather.4.cloned.1.call-done) | data formatting | bytes 7864320 | tf_op jit(solution)/shard_map/reshape | solution.py:99
  147.8 10.6 %bitcast_reduce_fusion = (f32[16,48,16]{1,2,0:T(8,128)S(1)}, f32[16,16,48,128]{3,2,1,0:T(8,128)}) fusion(pred[16,128]{1,0:T(8,128)(4,1)S(1)} %add_compare_fusion, bf16[16,128,16,80]{3,2,1,0:T(8,128)(2,1)} %reshape.1072, bf16[16,48,16,80]{3,2,1,0:T(8,128)(2,1)S(1)} %broadcast_select_fusion), kind=kOutput, calls=%fused_computation.15 | convolution fusion | flops 256364544 | bytes 13551616 | tf_op jit(solution)/shard_map/pqhd,pthd->pqht/dot_general | solution.py:104
  161.2 9.3 %fusion.23 = f32[16,48,16,80]{3,1,2,0:T(8,128)} fusion(bf16[16,128,16,80]{3,2,1,0:T(8,128)(2,1)} %reshape.1073, f32[16,16,48,128]{3,2,1,0:T(8,128)} %get-tuple-element.38, f32[16,48,16]{1,2,0:T(8,128)S(1)} %broadcast_select_fusion.1, pred[16,128]{1,0:T(8,128)(4,1)S(1)} %add_compare_fusion), kind=kOutput, calls=%fused_computation.37 | convolution fusion | flops 259522560 | bytes 15517696 | tf_op jit(solution)/shard_map/pqht,pthd->pqhd/dot_general | solution.py:112
  176.2 84.9 %all-reduce.2.cloned.1.call-done = f32[32,48,16]{1,0,2:T(8,128)} async-done(((f32[32,48,16]{1,0,2:T(8,128)}), f32[32,48,16]{1,0,2:T(8,128)}) %all-reduce.2.cloned.1.call-update) | async-done | bytes 98320 | tf_op jit(solution)/shard_map/pmax | solution.py:120
  263.7 13.1 %broadcast_multiply_fusion = f32[32,48,16,80]{3,0,2,1:T(8,128)} fusion(f32[32,48,16]{0,2,1:T(8,128)S(1)} %copy.110, f32[16,48,16,80]{3,1,2,0:T(8,128)} %fusion.23, s32[16]{0:T(128)S(1)} %convert_reduce_fusion), kind=kOutput, calls=%fused_computation.20 | convolution fusion | flops 379453952 | bytes 11894848 | tf_op jit(solution)/shard_map/pr,pqhd->rqhd/dot_general | solution.py:117
  276.9 16.4 %copy.111 = f32[32,48,16,80]{3,2,1,0:T(8,128)} copy(f32[32,48,16,80]{3,0,2,1:T(8,128)} %broadcast_multiply_fusion) | data formatting | bytes 15728640 | tf_op jit(solution)/shard_map/mul | solution.py:123
  293.3 12.8 %reshape.919 = f32[32,48,1280]{2,1,0:T(8,128)} reshape(f32[32,48,16,80]{3,2,1,0:T(8,128)} %copy.111) | data formatting | bytes 15728640 | tf_op jit(solution)/shard_map/reshape | solution.py:123
  313.2 26.5 %reduce-scatter.6.cloned.1.call-done = f32[1,48,16]{1,2,0:T(8,128)} async-done(((f32[32,48,16]{1,2,0:T(8,128)}), f32[1,48,16]{1,2,0:T(8,128)}) %reduce-scatter.6.cloned.1.call-update) | async-done | bytes 3088 | tf_op jit(solution)/shard_map/reduce_scatter | solution.py:127
  340.4 93.1 %reduce-scatter.4.cloned.1.call-done = f32[1,48,1280]{2,1,0:T(8,128)} async-done(((f32[32,48,1280]{2,1,0:T(8,128)}), f32[1,48,1280]{2,1,0:T(8,128)}) %reduce-scatter.4.cloned.1.call-update) | async-done | bytes 245776 | tf_op jit(solution)/shard_map/reduce_scatter | solution.py:128
  435.6 55.1 %all_to_all.67 = bf16[32,48,1280]{2,1,0:T(8,128)(2,1)S(1)} all-to-all(bf16[32,48,1280]{2,1,0:T(8,128)(2,1)S(1)} %stack.15), channel_id=1, replica_groups=mesh['req'=4,'blk'=32] {'blk'}, dimensions={0} | all-to-all | bytes 7864320 | tf_op jit(solution)/shard_map/all_to_all | solution.py:37
  492.9 11.3 %all_to_all.68 = bf16[32,2,960]{2,1,0:T(2,128)(2,1)S(1)} all-to-all(bf16[32,2,960]{2,1,0:T(2,128)(2,1)S(1)} %reshape.1081), channel_id=1, replica_groups=mesh['req'=4,'blk'=32] {'blk'}, dimensions={0} | all-to-all | bytes 245760 | tf_op jit(solution)/shard_map/all_to_all | solution.py:44
  505.4 51.8 %all_to_all.69 = bf16[32,48,1280]{2,1,0:T(8,128)(2,1)} all-to-all(bf16[32,48,1280]{2,1,0:T(8,128)(2,1)S(1)} %stack.16), channel_id=1, replica_groups=mesh['req'=4,'blk'=32] {'blk'}, dimensions={0} | all-to-all | bytes 7864320 | tf_op jit(solution)/shard_map/all_to_all | solution.py:37
  557.2 7.8 fusion.66
  565.0 86.5 %reduce-scatter.8.cloned.1.call-done = f32[48,1280]{1,0:T(8,128)} async-done(((f32[1536,1280]{1,0:T(8,128)}), f32[48,1280]{1,0:T(8,128)}) %reduce-scatter.8.cloned.1.call-update) | async-done | bytes 245776 | tf_op jit(solution)/shard_map/reduce_scatter | solution.py:167
  655.7 7.5 all-to-all-start.5
  669.6 59.5 %all-gather = bf16[32,5,2560]{2,1,0:T(8,128)(2,1)S(1)} all-gather(bf16[1,5,2560]{2,1,0:T(8,128)(2,1)S(1)} %fusion.12), channel_id=1, replica_groups=mesh['req'=4,'blk'=32] {'blk'}, dimensions={0}, use_global_device_ids=true | all-gather | bytes 844800 | tf_op jit(solution)/shard_map/all_gather | solution.py:206
  729.4 7.1 scatter_custom_fusion
  736.6 7.2 scatter_custom_fusion.1
  756.3 9.1 %maximum_bitcast_fusion = bf16[1,2,2048,1280]{3,2,1,0:T(8,128)(2,1)} fusion(bf16[1,2048,1280]{2,1,0:T(8,128)(2,1)} %bitcast.180, bf16[1,2048,1280]{2,1,0:T(8,128)(2,1)} %bitcast.181), kind=kLoop, calls=%fused_computation.9 | loop fusion | flops 5242880 | bytes 20971520 | tf_op jit(solution)/shard_map/broadcast_in_dim | solution.py:222
  (156 shorter events, 80.8 us)
Async XLA Ops:
  8.0 735.8 %copy-start = (bf16[4,1280,40]{1,2,0:T(8,128)(2,1)S(1)}, bf16[4,1280,40]{1,2,0:T(8,128)(2,1)}, u32[]{:S(2)}) copy-start(bf16[4,1280,40]{1,2,0:T(8,128)(2,1)} %param.25) | copy-start | bytes 1228804
  8.0 120.1 %all-gather.4.cloned.1.call-start = ((), (), s32[]{:S(2)}) async-start(), calls=%async_computation.10 | async-start | bytes 4055040 | tf_op jit(solution)/shard_map/all_gather | solution.py:77
  10.1 56.6 %copy-start.9 = (bf16[1280,120]{0,1:T(8,128)(2,1)S(1)}, bf16[1280,120]{0,1:T(8,128)(2,1)}, u32[]{:S(2)}) copy-start(bf16[1280,120]{0,1:T(8,128)(2,1)} %param.21) | copy-start | bytes 921604
  66.7 17.0 %copy-start.8 = (s32[1,32]{1,0:T(1,128)S(1)}, s32[1,32]{1,0:T(1,128)}, u32[]{:S(2)}) copy-start(s32[1,32]{1,0:T(1,128)} %param.18) | copy-start | bytes 388
  83.5 177.6 %all-reduce.2.cloned.1.call-start = ((), (), s32[]{:S(2)}) async-start(), calls=%async_computation.11 | async-start | bytes 524288 | tf_op jit(solution)/shard_map/pmax | solution.py:120
  110.3 15.8 %copy-start.1 = (s32[1,512]{1,0:T(1,128)S(1)}, s32[1,512]{1,0:T(1,128)}, u32[]{:S(2)}) copy-start(s32[1,512]{1,0:T(1,128)} %param.17) | copy-start | bytes 6148
  160.8 178.9 %reduce-scatter.6.cloned.1.call-start = ((), (), s32[]{:S(2)}) async-start(), calls=%async_computation.13 | async-start | bytes 270336 | tf_op jit(solution)/shard_map/reduce_scatter | solution.py:127
  263.7 169.8 %reduce-scatter.4.cloned.1.call-start = ((), (), s32[]{:S(2)}) async-start(), calls=%async_computation.12 | async-start | bytes 8110080 | tf_op jit(solution)/shard_map/reduce_scatter | solution.py:128
  306.1 0.7 copy-start.2
  306.1 345.5 %reduce-scatter.8.cloned.1.call-start = ((), (), s32[]{:S(2)}) async-start(), calls=%async_computation.14 | async-start | bytes 8110080 | tf_op jit(solution)/shard_map/reduce_scatter | solution.py:167
  435.4 55.4 %copy-start.5 = (bf16[1280,40]{0,1:T(8,128)(2,1)S(1)}, bf16[1280,40]{0,1:T(8,128)(2,1)}, u32[]{:S(2)}) copy-start(bf16[1280,40]{0,1:T(8,128)(2,1)} %param.22) | copy-start | bytes 307204
  490.7 14.2 %copy-start.3 = (bf16[48,1280]{1,0:T(8,128)(2,1)S(1)}, bf16[48,1280]{1,0:T(8,128)(2,1)}, u32[]{:S(2)}) copy-start(bf16[48,1280]{1,0:T(8,128)(2,1)} %param.15) | copy-start | bytes 368644
  505.2 52.1 %copy-start.6 = (bf16[40,1280]{1,0:T(8,128)(2,1)S(1)}, bf16[40,1280]{1,0:T(8,128)(2,1)}, u32[]{:S(2)}) copy-start(bf16[40,1280]{1,0:T(8,128)(2,1)} %param.24) | copy-start | bytes 307204
  505.2 52.1 %copy-start.7 = (bf16[1280,40]{0,1:T(8,128)(2,1)S(1)}, bf16[1280,40]{0,1:T(8,128)(2,1)}, u32[]{:S(2)}) copy-start(bf16[1280,40]{0,1:T(8,128)(2,1)} %param.23) | copy-start | bytes 307204
  653.3 2.4 copy-start.4
  655.7 8.1 %copy-start.10 = (s32[1,32]{1,0:T(1,128)S(1)}, s32[1,32]{1,0:T(1,128)}, u32[]{:S(2)}) copy-start(s32[1,32]{1,0:T(1,128)} %param.20) | copy-start | bytes 388
  655.7 88.1 %all-to-all-start.5 = ((bf16[32,48,1280]{2,1,0:T(8,128)(2,1)}), bf16[32,48,1280]{2,1,0:T(8,128)(2,1)}, u32[]{:S(2)}, u32[]{:S(2)}) async-start(bf16[32,48,1280]{2,1,0:T(8,128)(2,1)} %stack.17), calls=%async_computation.8 | async-start | bytes 7864320 | tf_op jit(solution)/shard_map/all_to_all | solution.py:37
  663.2 118.1 %all-gather.6.cloned.1.call-start = ((), (), s32[]{:S(2)}) async-start(), calls=%async_computation.15 | async-start | bytes 4096000 | tf_op jit(solution)/shard_map/all_gather | solution.py:195
  666.8 2.0 copy-start.11
  750.9 19.7 %all-to-all-start.6 = ((bf16[32,48,160]{2,1,0:T(8,128)(2,1)}), bf16[32,48,160]{2,1,0:T(8,128)(2,1)S(1)}, u32[]{:S(2)}, u32[]{:S(2)}) async-start(bf16[32,48,160]{2,1,0:T(8,128)(2,1)} %copy.123), calls=%async_computation.9 | async-start | bytes 1572864 | tf_op jit(solution)/shard_map/all_to_all | solution.py:44
Sparse Core Ops, SparseCore 0:
  83.6 44.4 all-gather.3
  160.9 100.1 all-reduce.1
  265.1 74.5 reduce-scatter.5
  343.9 89.5 reduce-scatter.3
  565.2 86.3 reduce-scatter.7
Sparse Core Ops, SparseCore 1:
  665.4 41.7 all-gather.5
